TPU v7x, 32 devices: a whole 2x2x4 slice. The times are simulated.
32 devices in a mesh: expert: 8 (over z, x), pair: 2 (over core), dp: 2 (over y).
Axes of the slice: x: 2, y: 2, z: 4, core: 2. Of those that a mesh axis runs over, the one named last changes fastest.
Arguments:
- tokens: bfloat16 [128, 196, 768], P(('expert', 'pair', 'dp')), may hold values from -96 to 96
- phi: bfloat16 [768, 16], replicated, may hold values from -0.25 to 0.25
- w_in: bfloat16 [8, 768, 3072], P('expert', None, 'pair'), may hold values from -0.21875 to 0.21875
- w_out: bfloat16 [8, 3072, 768], P('expert', 'pair'), may hold values from -0.109375 to 0.109375
- slot_out: bfloat16 [128, 16, 768], P(('expert', 'pair', 'dp')), may hold values from -6 to 6
- grad_out: bfloat16 [128, 196, 768], P(('expert', 'pair', 'dp')), may hold values from -6 to 6
Outputs:
- token_grad: bfloat16 [128, 196, 768], P(('expert', 'pair', 'dp'))
- phi_grad: float32 [768, 16], replicated
- grad_w_in: bfloat16 [8, 768, 3072], P('expert', 'dp', 'pair')
- grad_w_out: bfloat16 [8, 3072, 768], P('expert', 'pair', 'dp')
All inputs are finite; a program needn't handle non-finite values.
Results may differ from a plain program's by a relative error of at most 0.0086.
Values may be sent and summed in bfloat16 or wider, within the bound.
A program may use at most 128 MiB of HBM per device.

v0:
```python
import jax
import jax.numpy as jnp
from jax import lax
from jax.sharding import PartitionSpec as P


def expert_rows(z_rows, g_rows, w_first, w_second):
    pre = jnp.dot(z_rows, w_first, preferred_element_type=jnp.float32)
    act_full, gelu_back = jax.vjp(jax.nn.gelu, pre)
    act = act_full.astype(jnp.bfloat16)
    dact = lax.dot_general(
        g_rows, w_second, (((1,), (1,)), ((), ())), preferred_element_type=jnp.float32
    )
    dpre = gelu_back(dact)[0].astype(jnp.bfloat16)
    grad_second = lax.dot_general(
        act, g_rows, (((0,), (0,)), ((), ())), preferred_element_type=jnp.float32
    )
    grad_first = lax.dot_general(
        z_rows, dpre, (((0,), (0,)), ((), ())), preferred_element_type=jnp.float32
    )
    back = lax.dot_general(
        dpre, w_first, (((1,), (1,)), ((), ())), preferred_element_type=jnp.float32
    )
    return (grad_first, grad_second, back)


def local(tokens, phi, w_in, w_out, slot_out, grad_out):
    f32 = jnp.float32
    images, _, width = tokens.shape
    groups = lax.axis_size("expert")
    per_group = phi.shape[1] // groups
    experts_here = w_in.shape[0]
    slots = per_group // experts_here
    logits = jnp.einsum("bmd,ds->bms", tokens, phi, preferred_element_type=f32)
    dispatch = jax.nn.softmax(logits, axis=1)
    combine = jax.nn.softmax(logits, axis=2)
    dispatch_low = dispatch.astype(jnp.bfloat16)
    combine_low = combine.astype(jnp.bfloat16)
    slot_in = jnp.einsum("bms,bmd->bsd", dispatch_low, tokens, preferred_element_type=f32).astype(
        jnp.bfloat16
    )
    slot_grad = jnp.einsum(
        "bms,bmd->bsd", combine_low, grad_out, preferred_element_type=f32
    ).astype(jnp.bfloat16)
    outgoing_in = slot_in.reshape(images, groups, per_group, width)
    outgoing_grad = slot_grad.reshape(images, groups, per_group, width)
    arrived_in, arrived_grad = (
        lax.all_to_all(outgoing_in, "expert", split_axis=1, concat_axis=0, tiled=True),
        lax.all_to_all(outgoing_grad, "expert", split_axis=1, concat_axis=0, tiled=True),
    )
    rows_in, rows_grad = (
        lax.all_gather(arrived_in, "pair", axis=0, tiled=True),
        lax.all_gather(arrived_grad, "pair", axis=0, tiled=True),
    )
    count = rows_in.shape[0]
    z_rows = rows_in[:, 0].reshape(count * slots, width)
    g_rows = rows_grad[:, 0].reshape(count * slots, width)
    grad_first, grad_second, back = expert_rows(z_rows, g_rows, w_in[0], w_out[0])
    firsts = [grad_first]
    seconds = [grad_second]
    backs = back.reshape(count, 1, slots, width)
    back_sum = lax.psum_scatter(backs, "pair", scatter_dimension=0, tiled=True)
    grad_w_in = lax.psum_scatter(
        jnp.stack(firsts).astype(jnp.bfloat16), "dp", scatter_dimension=1, tiled=True
    )
    grad_w_out = lax.psum_scatter(
        jnp.stack(seconds).astype(jnp.bfloat16), "dp", scatter_dimension=2, tiled=True
    )
    back_low = back_sum.astype(jnp.bfloat16)
    returned = lax.all_to_all(back_low, "expert", split_axis=0, concat_axis=1, tiled=True)
    slot_in_grad = returned.reshape(images, groups * per_group, width)
    dispatch_grad = jnp.einsum("bmd,bsd->bms", tokens, slot_in_grad, preferred_element_type=f32)
    combine_grad = jnp.einsum("bmd,bsd->bms", grad_out, slot_out, preferred_element_type=f32)
    logit_grad = dispatch * (
        dispatch_grad - jnp.sum(dispatch * dispatch_grad, axis=1, keepdims=True)
    )
    logit_grad = logit_grad + combine * (
        combine_grad - jnp.sum(combine * combine_grad, axis=2, keepdims=True)
    )
    logit_low = logit_grad.astype(jnp.bfloat16)
    token_part = jnp.einsum("bms,bsd->bmd", dispatch_low, slot_in_grad, preferred_element_type=f32)
    token_grad = (
        token_part + jnp.einsum("bms,ds->bmd", logit_low, phi, preferred_element_type=f32)
    ).astype(jnp.bfloat16)
    phi_part = jnp.einsum("bmd,bms->ds", tokens, logit_low, preferred_element_type=f32)
    phi_grad = lax.psum(phi_part, ("expert", "pair", "dp"))
    return (token_grad, phi_grad, grad_w_in, grad_w_out)


def solution(mesh):
    in_specs = (
        P(("expert", "pair", "dp"), None, None),
        P(),
        P("expert", None, "pair"),
        P("expert", "pair", None),
        P(("expert", "pair", "dp"), None, None),
        P(("expert", "pair", "dp"), None, None),
    )
    out_specs = (
        P(("expert", "pair", "dp"), None, None),
        P(),
        P("expert", "dp", "pair"),
        P("expert", "pair", "dp"),
    )
    return jax.shard_map(local, mesh=mesh, in_specs=in_specs, out_specs=out_specs, check_vma=False)
```

profile of v0, /device:TPU:0, one launch (start us, length us, event | category | flops | bytes accessed | tf_op | source)
XLA Modules:
  0.0 153.0 jit_solution(3510893113097627227)
XLA Ops:
  7.2 1.8 %fusion.32 = f32[4,196,16]{1,2,0:T(8,128)S(1)} fusion(bf16[4,196,768]{2,0,1:T(4,128)(2,1)} %param.6, bf16[768,16]{0,1:T(8,128)(2,1)} %param.7), kind=kOutput, calls=%fused_computation.41 | convolution fusion | flops 19267584 | bytes 1278976 | tf_op jit(solution)/shard_map/bmd,ds->bms/dot_general | solution.py:34
  12.1 7.3 %all-to-all-start = ((bf16[4,8,2,768]{3,2,0,1:T(2,128)(2,1)}), bf16[4,8,2,768]{3,2,0,1:T(2,128)(2,1)S(1)}, u32[]{:S(2)}, u32[]{:S(2)}) async-start(bf16[4,8,2,768]{3,2,0,1:T(2,128)(2,1)} %copy.32), calls=%async_computation | async-start | bytes 196608 | tf_op jit(solution)/shard_map/all_to_all | solution.py:49
  22.4 4.0 %all-to-all-done = bf16[4,8,2,768]{3,2,0,1:T(2,128)(2,1)S(1)} async-done(((bf16[4,8,2,768]{3,2,0,1:T(2,128)(2,1)}), bf16[4,8,2,768]{3,2,0,1:T(2,128)(2,1)S(1)}, u32[]{:S(2)}, u32[]{:S(2)}) %all-to-all-start) | async-done | bytes 98336 | tf_op jit(solution)/shard_map/all_to_all | solution.py:49
  26.5 3.4 %all-to-all-start.1 = ((bf16[4,8,2,768]{3,2,0,1:T(2,128)(2,1)}), bf16[4,8,2,768]{3,2,0,1:T(2,128)(2,1)S(1)}, u32[]{:S(2)}, u32[]{:S(2)}) async-start(bf16[4,8,2,768]{3,2,0,1:T(2,128)(2,1)} %copy.35), calls=%async_computation.1 | async-start | bytes 196608 | tf_op jit(solution)/shard_map/all_to_all | solution.py:48
  29.9 1.9 %all_gather.6 = bf16[64,1,2,768]{3,2,1,0:T(2,128)(2,1)S(1)} all-gather(bf16[32,1,2,768]{3,2,1,0:T(2,128)(2,1)S(1)} %bitcast.73), channel_id=1, replica_groups=mesh['expert'=8,'pair'=2,'dp'=2] {'pair'}, dimensions={0}, use_global_device_ids=true | all-gather | bytes 294912 | tf_op jit(solution)/shard_map/all_gather | solution.py:53
  31.9 5.0 %all-to-all-done.1 = bf16[4,8,2,768]{3,2,0,1:T(2,128)(2,1)S(1)} async-done(((bf16[4,8,2,768]{3,2,0,1:T(2,128)(2,1)}), bf16[4,8,2,768]{3,2,0,1:T(2,128)(2,1)S(1)}, u32[]{:S(2)}, u32[]{:S(2)}) %all-to-all-start.1) | async-done | bytes 98336 | tf_op jit(solution)/shard_map/all_to_all | solution.py:48
  36.9 1.9 %all_gather.7 = bf16[64,1,2,768]{3,2,1,0:T(2,128)(2,1)S(1)} all-gather(bf16[32,1,2,768]{3,2,1,0:T(2,128)(2,1)S(1)} %bitcast.74), channel_id=1, replica_groups=mesh['expert'=8,'pair'=2,'dp'=2] {'pair'}, dimensions={0}, use_global_device_ids=true | all-gather | bytes 294912 | tf_op jit(solution)/shard_map/all_gather | solution.py:52
  40.6 1.8 %fusion.40 = bf16[128,1536]{1,0:T(8,128)(2,1)} fusion(f32[128,1536]{1,0:T(8,128)S(1)} %fusion.8, bf16[128,768]{1,0:T(8,128)(2,1)S(1)} %reshape_squeeze.6, bf16[1,1536,768]{2,1,0:T(8,128)(2,1)S(1)} %copy-done.7), kind=kOutput, calls=%fused_computation.49 | convolution fusion | flops 305922048 | bytes 3735552 | tf_op jit(solution)/shard_map/dot_general | solution.py:11
  42.4 1.9 %reshape.35 = bf16[64,2,1536]{2,1,0:T(2,128)(2,1)} reshape(bf16[128,1536]{1,0:T(8,128)(2,1)} %fusion.40) | data formatting | bytes 786432 | tf_op jit(solution)/shard_map/reshape.16
  44.3 2.6 %fusion.12 = f32[64,1,2,768]{3,0,2,1:T(8,128)} fusion(bf16[1,768,1536]{2,1,0:T(8,128)(2,1)S(1)} %copy-done, bf16[64,2,1536]{2,1,0:T(2,128)(2,1)} %reshape.35), kind=kOutput, calls=%fused_computation.17 | convolution fusion | flops 301989888 | bytes 3145728 | tf_op jit(solution)/shard_map/dot_general | solution.py:21
  47.0 2.3 %fusion.5 = bf16[1,1536,768]{2,1,0:T(8,128)(2,1)} fusion(bf16[128,768]{1,0:T(8,128)(2,1)S(1)} %reshape_squeeze.6, f32[128,1536]{1,0:T(8,128)S(1)} %fusion.8), kind=kOutput, calls=%fused_computation.7 | convolution fusion | flops 304939008 | bytes 3342336 | tf_op jit(solution)/shard_map/dot_general | solution.py:15
  49.3 12.2 %copy.44 = bf16[1,1536,768]{1,0,2:T(2,128)(2,1)} copy(bf16[1,1536,768]{2,1,0:T(8,128)(2,1)} %fusion.5) | data formatting | bytes 4718592
  61.5 4.4 %copy.63 = bf16[768,1,1536]{2,0,1:T(8,128)(2,1)} copy(bf16[768,1,1536]{2,1,0:T(2,128)(2,1)} %bitcast.69) | data formatting | bytes 4718592
  66.8 2.2 %fusion.4 = bf16[1,768,1536]{2,1,0:T(8,128)(2,1)} fusion(bf16[128,768]{1,0:T(8,128)(2,1)S(1)} %reshape_squeeze.7, bf16[128,1536]{1,0:T(8,128)(2,1)S(1)} %copy-done.1), kind=kOutput, calls=%fused_computation.6 | convolution fusion | flops 303169536 | bytes 2949120 | tf_op jit(solution)/shard_map/dot_general | solution.py:18
  70.0 1.8 %fusion.25 = f32[4,196,16]{1,2,0:T(8,128)S(1)} fusion(bf16[4,16,768]{2,1,0:T(8,128)(2,1)S(1)} %copy-done.8, bf16[4,196,768]{2,0,1:T(4,128)(2,1)} %param.11), kind=kOutput, calls=%fused_computation.34 | convolution fusion | flops 19267584 | bytes 1352704 | tf_op jit(solution)/shard_map/bmd,bsd->bms/dot_general | solution.py:73
  73.5 3.5 %all-to-all-start.2 = ((bf16[32,1,2,768]{3,2,1,0:T(2,128)(2,1)}), bf16[32,1,2,768]{3,2,1,0:T(2,128)(2,1)S(1)}, u32[]{:S(2)}, u32[]{:S(2)}) async-start(bf16[32,1,2,768]{3,2,1,0:T(2,128)(2,1)} %copy.38), calls=%async_computation.3 | async-start | bytes 196608 | tf_op jit(solution)/shard_map/all_to_all | solution.py:70
  77.3 6.8 %all-to-all-done.2 = bf16[32,1,2,768]{3,2,1,0:T(2,128)(2,1)S(1)} async-done(((bf16[32,1,2,768]{3,2,1,0:T(2,128)(2,1)}), bf16[32,1,2,768]{3,2,1,0:T(2,128)(2,1)S(1)}, u32[]{:S(2)}, u32[]{:S(2)}) %all-to-all-start.2) | async-done | bytes 98336 | tf_op jit(solution)/shard_map/all_to_all | solution.py:70
  86.0 2.2 %fusion.28 = f32[4,196,768]{2,1,0:T(8,128)} fusion(f32[4,196,16]{1,2,0:T(8,128)S(1)} %fusion.23, f32[4,196,16]{1,2,0:T(8,128)S(1)} %convolution_bitcast_fusion, bf16[768,16]{0,1:T(8,128)(2,1)S(1)} %copy-done.6, f32[4,196,16]{1,2,0:T(8,128)S(1)} %copy-done.4, f32[4,16]{1,0:T(4,128)S(1)} %get-tuple-element.18), kind=kOutput, calls=%fused_computation.37 | convolution fusion | flops 19355652 | bytes 2583808 | tf_op jit(solution)/shard_map/bms,ds->bmd/dot_general | solution.py:83
  88.1 3.6 %add_convert_fusion = bf16[4,196,768]{2,1,0:T(8,128)(2,1)} fusion(f32[4,196,768]{2,1,0:T(8,128)} %fusion.28, bf16[4,16,768]{2,1,0:T(8,128)(2,1)S(1)} %reshape.36, f32[4,16]{1,0:T(4,128)S(1)} %get-tuple-element.18, f32[4,196,16]{1,2,0:T(8,128)S(1)} %copy-done.3), kind=kOutput, calls=%fused_computation.8 | convolution fusion | flops 20509700 | bytes 3761408 | tf_op jit(solution)/shard_map/bms,bsd->bmd/dot_general | solution.py:81
  91.7 2.8 %copy.43 = bf16[4,196,768]{2,0,1:T(4,128)(2,1)} copy(bf16[4,196,768]{2,1,0:T(8,128)(2,1)} %add_convert_fusion) | data formatting | bytes 2408448
  94.6 1.7 %convolution_bitcast_fusion.1 = f32[768,16]{0,1:T(8,128)S(1)} fusion(f32[4,196,16]{1,2,0:T(8,128)S(1)} %fusion.23, f32[4,196,16]{1,2,0:T(8,128)S(1)} %convolution_bitcast_fusion, bf16[4,196,768]{2,0,1:T(4,128)(2,1)} %param.6, f32[4,196,16]{1,2,0:T(8,128)S(1)} %copy-done.4, f32[4,16]{1,0:T(4,128)S(1)} %get-tuple-element.18), kind=kOutput, calls=%fused_computation.33 | convolution fusion | flops 19355652 | bytes 1404160 | tf_op jit(solution)/shard_map/bmd,bms->ds/dot_general | solution.py:85
  96.3 39.8 %psum.7 = f32[768,16]{0,1:T(8,128)} all-reduce(f32[768,16]{0,1:T(8,128)S(1)} %convolution_bitcast_fusion.1), channel_id=1, replica_groups=mesh['expert'=8,'pair'=2,'dp'=2] {'expert','pair','dp'}, use_global_device_ids=true, to_apply=%region_7.0 | all-reduce | flops 12288 | bytes 98304 | tf_op jit(solution)/shard_map/psum | solution.py:86
  136.1 3.9 %reshape_bitcast_fusion = bf16[1,1536,384]{1,0,2:T(2,128)(2,1)} fusion(bf16[384,1536]{1,0:T(8,128)(2,1)} %reduce-scatter.10.cloned.1.call-done), kind=kLoop, calls=%fused_computation.10 | loop fusion | bytes 2359296
  140.1 6.4 %copy.45 = bf16[1,1536,384]{2,1,0:T(8,128)(2,1)} copy(bf16[1,1536,384]{1,0,2:T(2,128)(2,1)} %reshape_bitcast_fusion) | data formatting | bytes 2359296
  (44 shorter events, 13.7 us)
Async XLA Ops:
  7.2 31.8 %copy-start = (bf16[1,768,1536]{2,1,0:T(8,128)(2,1)S(1)}, bf16[1,768,1536]{2,1,0:T(8,128)(2,1)}, u32[]{:S(2)}) copy-start(bf16[1,768,1536]{2,1,0:T(8,128)(2,1)} %param.8) | copy-start | bytes 7077892
  9.0 12.7 %copy-start.2 = (f32[4,196,16]{1,2,0:T(8,128)}, f32[4,196,16]{1,2,0:T(8,128)S(1)}, u32[]{:S(2)}) copy-start(f32[4,196,16]{1,2,0:T(8,128)S(1)} %fusion.32) | copy-start | bytes 150532
  12.1 14.4 %all-to-all-start = ((bf16[4,8,2,768]{3,2,0,1:T(2,128)(2,1)}), bf16[4,8,2,768]{3,2,0,1:T(2,128)(2,1)S(1)}, u32[]{:S(2)}, u32[]{:S(2)}) async-start(bf16[4,8,2,768]{3,2,0,1:T(2,128)(2,1)} %copy.32), calls=%async_computation | async-start | bytes 196608 | tf_op jit(solution)/shard_map/all_to_all | solution.py:49
  26.5 10.4 %all-to-all-start.1 = ((bf16[4,8,2,768]{3,2,0,1:T(2,128)(2,1)}), bf16[4,8,2,768]{3,2,0,1:T(2,128)(2,1)S(1)}, u32[]{:S(2)}, u32[]{:S(2)}) async-start(bf16[4,8,2,768]{3,2,0,1:T(2,128)(2,1)} %copy.35), calls=%async_computation.1 | async-start | bytes 196608 | tf_op jit(solution)/shard_map/all_to_all | solution.py:48
  29.8 42.0 %reduce-scatter.6.cloned.1.call-start = ((), (), s32[]{:S(2)}) async-start(), calls=%async_computation.6 | async-start | bytes 589824 | tf_op jit(solution)/shard_map/reduce_scatter | solution.py:62
  38.9 1.7 %copy-start.7 = (bf16[1,1536,768]{2,1,0:T(8,128)(2,1)S(1)}, bf16[1,1536,768]{2,1,0:T(8,128)(2,1)}, u32[]{:S(2)}) copy-start(bf16[1,1536,768]{2,1,0:T(8,128)(2,1)} %param.9) | copy-start | bytes 7077892
  46.9 89.2 %reduce-scatter.10.cloned.1.call-start = ((), (), s32[]{:S(2)}) async-start(), calls=%async_computation.8 | async-start | bytes 3538944
  65.8 1.0 copy-start.1
  65.9 80.6 %reduce-scatter.8.cloned.1.call-start = ((), (), s32[]{:S(2)}) async-start(), calls=%async_computation.7 | async-start | bytes 3538944 | tf_op jit(solution)/shard_map/reduce_scatter | solution.py:63
  69.1 0.9 copy-start.8
  70.0 7.1 %copy-start.5 = (f32[4,196,16]{1,2,0:T(8,128)S(1)}, f32[4,196,16]{1,2,0:T(8,128)}, u32[]{:S(2)}) copy-start(f32[4,196,16]{1,2,0:T(8,128)} %get-tuple-element.17) | copy-start | bytes 150532
  73.5 12.4 %copy-start.4 = (f32[4,196,16]{1,2,0:T(8,128)S(1)}, f32[4,196,16]{1,2,0:T(8,128)}, u32[]{:S(2)}) copy-start(f32[4,196,16]{1,2,0:T(8,128)} %get-tuple-element.19) | copy-start | bytes 150532
  73.5 12.4 %copy-start.6 = (bf16[768,16]{0,1:T(8,128)(2,1)S(1)}, bf16[768,16]{0,1:T(8,128)(2,1)}, u32[]{:S(2)}) copy-start(bf16[768,16]{0,1:T(8,128)(2,1)} %param.7) | copy-start | bytes 73732
  73.5 10.6 %all-to-all-start.2 = ((bf16[32,1,2,768]{3,2,1,0:T(2,128)(2,1)}), bf16[32,1,2,768]{3,2,1,0:T(2,128)(2,1)S(1)}, u32[]{:S(2)}, u32[]{:S(2)}) async-start(bf16[32,1,2,768]{3,2,1,0:T(2,128)(2,1)} %copy.38), calls=%async_computation.3 | async-start | bytes 196608 | tf_op jit(solution)/shard_map/all_to_all | solution.py:70
  85.9 2.2 %copy-start.3 = (f32[4,196,16]{1,2,0:T(8,128)S(1)}, f32[4,196,16]{1,2,0:T(8,128)}, u32[]{:S(2)}) copy-start(f32[4,196,16]{1,2,0:T(8,128)} %copy-done.2) | copy-start | bytes 150532
Sparse Core Ops, SparseCore 0:
  47.1 5.4 reduce-scatter.5
  66.0 32.4 reduce-scatter.9
  101.3 35.5 reduce-scatter.7
where the time goes:
time: 154 us; the launch traced here: 153 us
  blocking collectives  43.7 us (28%)
  local copies, waits for them, and re-layouts  37.2 us (24%)
  matrix products  25.5 us (17%)
  waiting for transfers between devices  15.9 us (10%)
  starting transfers between devices  14.3 us (9%)
  between operations  13.9 us (9%)
  other arithmetic  2.6 us (2%)
    psum x1, blocking collectives, local(): phi_grad = lax.psum(phi_part, ('expert', 'pair', 'dp'))  39.8 us
    unnamed x23, local copies, waits for them, and re-layouts  32.8 us
    all_to_all x1, starting transfers between devices, local(): lax.all_to_all(outgoing_grad, 'expert', split_axis=1, concat_axis=0, tile...  7.28 us
    all_to_all x1, waiting for transfers between devices, local(): lax.all_to_all(back_low, 'expert', split_axis=0, concat_axis=1, tiled=True)  6.84 us
    all_to_all x1, waiting for transfers between devices, local(): lax.all_to_all(outgoing_in, 'expert', split_axis=1, concat_axis=0, tiled=...  4.98 us
    all_to_all x1, waiting for transfers between devices, local(): lax.all_to_all(outgoing_grad, 'expert', split_axis=1, concat_axis=0, tile...  4.02 us
    dot_general x1, matrix products, local(): jnp.einsum('bms,bsd->bmd', dispatch_low, slot_in_grad, preferred_element_...  3.6 us
    all_to_all x1, starting transfers between devices, local(): lax.all_to_all(back_low, 'expert', split_axis=0, concat_axis=1, tiled=True)  3.49 us
  transfers between devices with their start and end apart: 6, of which 3 were waited for; matrix products, arithmetic and copies ran while one was open for 33% of the time, Pallas kernels for 0%

commit v1 on v0

--- a/solution.py
+++ b/solution.py
@@ -83,7 +83,7 @@
         token_part + jnp.einsum("bms,ds->bmd", logit_low, phi, preferred_element_type=f32)
     ).astype(jnp.bfloat16)
     phi_part = jnp.einsum("bmd,bms->ds", tokens, logit_low, preferred_element_type=f32)
-    phi_grad = lax.psum(phi_part, ("expert", "pair", "dp"))
+    phi_grad = jnp.sum(lax.all_gather(phi_part, ("expert", "pair", "dp")), axis=0)
     return (token_grad, phi_grad, grad_w_in, grad_w_out)
 
 

time: 154 us -> 171 us (1.11)
  waiting for transfers between devices: 15.9 us -> 62.5 us
  blocking collectives: 43.7 us -> 3.88 us
  matrix products: 25.5 us -> 27.9 us
  starting transfers between devices: 14.3 us -> 16.5 us
  other arithmetic: 2.6 us -> 4.67 us
    psum x1 -> x0, blocking collectives: 39.8 us -> none  [local(): phi_grad = lax.psum(phi_part, ('expert', 'pair', 'dp'))]
    all_gather x0 -> x1, waiting for transfers between devices: none -> 30.5 us  [local(): lax.all_gather(phi_part, ('expert', 'pair', 'dp'))]
    reduce_scatter x1, waiting for transfers between devices: 0.01 us -> 14.2 us  [local(): lax.psum_scatter(jnp.stack(firsts).astype(jnp.bfloat16), 'dp', scatter_di...]
    reduce_scatter x1, waiting for transfers between devices: 0.01 us -> 3.23 us  [local(): back_sum = lax.psum_scatter(backs, 'pair', scatter_dimension=0, tiled=True)]
    all_to_all x1, starting transfers between devices: 3.49 us -> 5.72 us  [local(): lax.all_to_all(back_low, 'expert', split_axis=0, concat_axis=1, tiled=True)]
    unnamed x23 -> x28, local copies, waits for them, and re-layouts: 32.8 us -> 34.5 us
  transfers between devices with their start and end apart: 6 -> 7, of which waited for: 3 -> 6; matrix products, arithmetic and copies ran while one was open for 33% -> 30% of each run, Pallas kernels for 0% -> 0%
where the time goes in v1:
time: 171 us; the launch traced here: 170 us
  waiting for transfers between devices  62.5 us (37%)
  local copies, waits for them, and re-layouts  38.9 us (23%)
  matrix products  27.9 us (16%)
  starting transfers between devices  16.5 us (10%)
  between operations  15.6 us (9%)
  other arithmetic  4.67 us (3%)
  blocking collectives  3.88 us (2%)
    unnamed x28, local copies, waits for them, and re-layouts  34.5 us
    all_gather x1, waiting for transfers between devices, local(): lax.all_gather(phi_part, ('expert', 'pair', 'dp'))  30.5 us
    reduce_scatter x1, waiting for transfers between devices, local(): lax.psum_scatter(jnp.stack(firsts).astype(jnp.bfloat16), 'dp', scatter_di...  14.2 us
    all_to_all x1, starting transfers between devices, local(): lax.all_to_all(outgoing_grad, 'expert', split_axis=1, concat_axis=0, tile...  7.28 us
    all_to_all x1, starting transfers between devices, local(): lax.all_to_all(back_low, 'expert', split_axis=0, concat_axis=1, tiled=True)  5.72 us
    all_to_all x1, waiting for transfers between devices, local(): lax.all_to_all(back_low, 'expert', split_axis=0, concat_axis=1, tiled=True)  5.49 us
    all_to_all x1, waiting for transfers between devices, local(): lax.all_to_all(outgoing_in, 'expert', split_axis=1, concat_axis=0, tiled=...  4.97 us
    all_to_all x1, waiting for transfers between devices, local(): lax.all_to_all(outgoing_grad, 'expert', split_axis=1, concat_axis=0, tile...  4.03 us
  transfers between devices with their start and end apart: 7, of which 6 were waited for; matrix products, arithmetic and copies ran while one was open for 30% of the time, Pallas kernels for 0%

profile of v1, /device:TPU:0, one launch (start us, length us, event | category | flops | bytes accessed | tf_op | source)
XLA Modules:
  0.0 170.0 jit_solution(16575623760961690871)
XLA Ops:
  12.9 7.3 %all-to-all-start = ((bf16[4,8,2,768]{3,2,0,1:T(2,128)(2,1)}), bf16[4,8,2,768]{3,2,0,1:T(2,128)(2,1)S(1)}, u32[]{:S(2)}, u32[]{:S(2)}) async-start(bf16[4,8,2,768]{3,2,0,1:T(2,128)(2,1)} %copy.32), calls=%async_computation | async-start | bytes 196608 | tf_op jit(solution)/shard_map/all_to_all | solution.py:49
  23.3 4.0 %all-to-all-done = bf16[4,8,2,768]{3,2,0,1:T(2,128)(2,1)S(1)} async-done(((bf16[4,8,2,768]{3,2,0,1:T(2,128)(2,1)}), bf16[4,8,2,768]{3,2,0,1:T(2,128)(2,1)S(1)}, u32[]{:S(2)}, u32[]{:S(2)}) %all-to-all-start) | async-done | bytes 98336 | tf_op jit(solution)/shard_map/all_to_all | solution.py:49
  27.3 3.4 %all-to-all-start.1 = ((bf16[4,8,2,768]{3,2,0,1:T(2,128)(2,1)}), bf16[4,8,2,768]{3,2,0,1:T(2,128)(2,1)S(1)}, u32[]{:S(2)}, u32[]{:S(2)}) async-start(bf16[4,8,2,768]{3,2,0,1:T(2,128)(2,1)} %copy.35), calls=%async_computation.1 | async-start | bytes 196608 | tf_op jit(solution)/shard_map/all_to_all | solution.py:48
  30.7 1.9 %all_gather.12 = bf16[64,1,2,768]{3,2,1,0:T(2,128)(2,1)S(1)} all-gather(bf16[32,1,2,768]{3,2,1,0:T(2,128)(2,1)S(1)} %bitcast.79), channel_id=1, replica_groups=mesh['expert'=8,'pair'=2,'dp'=2] {'pair'}, dimensions={0}, use_global_device_ids=true | all-gather | bytes 294912 | tf_op jit(solution)/shard_map/all_gather | solution.py:53
  32.8 5.0 %all-to-all-done.1 = bf16[4,8,2,768]{3,2,0,1:T(2,128)(2,1)S(1)} async-done(((bf16[4,8,2,768]{3,2,0,1:T(2,128)(2,1)}), bf16[4,8,2,768]{3,2,0,1:T(2,128)(2,1)S(1)}, u32[]{:S(2)}, u32[]{:S(2)}) %all-to-all-start.1) | async-done | bytes 98336 | tf_op jit(solution)/shard_map/all_to_all | solution.py:48
  37.7 1.9 %all_gather.13 = bf16[64,1,2,768]{3,2,1,0:T(2,128)(2,1)S(1)} all-gather(bf16[32,1,2,768]{3,2,1,0:T(2,128)(2,1)S(1)} %bitcast.80), channel_id=1, replica_groups=mesh['expert'=8,'pair'=2,'dp'=2] {'pair'}, dimensions={0}, use_global_device_ids=true | all-gather | bytes 294912 | tf_op jit(solution)/shard_map/all_gather | solution.py:52
  43.2 1.9 %reshape.35 = bf16[64,2,1536]{2,1,0:T(2,128)(2,1)} reshape(bf16[128,1536]{1,0:T(8,128)(2,1)} %fusion.40) | data formatting | bytes 786432 | tf_op jit(solution)/shard_map/reshape.16
  45.1 2.7 %fusion.12 = f32[64,1,2,768]{3,0,2,1:T(8,128)} fusion(bf16[1,768,1536]{2,1,0:T(8,128)(2,1)S(1)} %copy-done, bf16[64,2,1536]{2,1,0:T(2,128)(2,1)} %reshape.35), kind=kOutput, calls=%fused_computation.18 | convolution fusion | flops 301989888 | bytes 3145728 | tf_op jit(solution)/shard_map/dot_general | solution.py:21
  47.8 2.4 %fusion.25 = f32[4,196,16]{1,2,0:T(8,128)} fusion(bf16[4,16,768]{2,1,0:T(8,128)(2,1)S(1)} %copy-done.10, bf16[4,196,768]{2,0,1:T(4,128)(2,1)} %param.11), kind=kOutput, calls=%fused_computation.35 | convolution fusion | flops 19267584 | bytes 1352704 | tf_op jit(solution)/shard_map/bmd,bsd->bms/dot_general | solution.py:73
  50.2 3.2 %reduce-scatter.6.cloned.1.call-done = f32[32,1,2,768]{3,0,2,1:T(8,128)} async-done(((f32[64,1,2,768]{3,0,2,1:T(8,128)}), f32[32,1,2,768]{3,0,2,1:T(8,128)}) %reduce-scatter.6.cloned.1.call-update) | async-done | bytes 196624 | tf_op jit(solution)/shard_map/reduce_scatter | solution.py:62
  55.1 5.7 %all-to-all-start.2 = ((bf16[32,1,2,768]{3,2,1,0:T(2,128)(2,1)}), bf16[32,1,2,768]{3,2,1,0:T(2,128)(2,1)S(1)}, u32[]{:S(2)}, u32[]{:S(2)}) async-start(bf16[32,1,2,768]{3,2,1,0:T(2,128)(2,1)} %copy.38), calls=%async_computation.3 | async-start | bytes 196608 | tf_op jit(solution)/shard_map/all_to_all | solution.py:70
  62.4 5.5 %all-to-all-done.2 = bf16[32,1,2,768]{3,2,1,0:T(2,128)(2,1)S(1)} async-done(((bf16[32,1,2,768]{3,2,1,0:T(2,128)(2,1)}), bf16[32,1,2,768]{3,2,1,0:T(2,128)(2,1)S(1)}, u32[]{:S(2)}, u32[]{:S(2)}) %all-to-all-start.2) | async-done | bytes 98336 | tf_op jit(solution)/shard_map/all_to_all | solution.py:70
  69.7 2.5 %convolution_bitcast_fusion.1 = f32[768,16]{0,1:T(8,128)} fusion(f32[4,196,16]{1,2,0:T(8,128)} %fusion.23, f32[4,196,16]{1,2,0:T(8,128)S(1)} %convolution_bitcast_fusion, bf16[4,196,768]{2,0,1:T(4,128)(2,1)} %param.6, f32[4,196,16]{1,2,0:T(8,128)} %get-tuple-element.19, f32[4,16]{1,0:T(4,128)S(1)} %get-tuple-element.18), kind=kOutput, calls=%fused_computation.34 | convolution fusion | flops 19355652 | bytes 1404160 | tf_op jit(solution)/shard_map/bmd,bms->ds/dot_general | solution.py:85
  72.4 3.3 %fusion.5 = bf16[1,1536,768]{2,1,0:T(8,128)(2,1)} fusion(bf16[128,768]{1,0:T(8,128)(2,1)} %copy-done.2, f32[128,1536]{1,0:T(8,128)S(1)} %fusion.8), kind=kOutput, calls=%fused_computation.7 | convolution fusion | flops 304939008 | bytes 3342336 | tf_op jit(solution)/shard_map/dot_general | solution.py:15
  75.6 12.2 %copy.44 = bf16[1,1536,768]{1,0,2:T(2,128)(2,1)} copy(bf16[1,1536,768]{2,1,0:T(8,128)(2,1)} %fusion.5) | data formatting | bytes 4718592
  87.8 4.4 %copy.64 = bf16[768,1,1536]{2,0,1:T(8,128)(2,1)} copy(bf16[768,1,1536]{2,1,0:T(2,128)(2,1)} %bitcast.74) | data formatting | bytes 4718592
  93.1 2.2 %fusion.4 = bf16[1,768,1536]{2,1,0:T(8,128)(2,1)} fusion(bf16[128,768]{1,0:T(8,128)(2,1)S(1)} %reshape_squeeze.7, bf16[128,1536]{1,0:T(8,128)(2,1)S(1)} %copy-done.1), kind=kOutput, calls=%fused_computation.6 | convolution fusion | flops 303169536 | bytes 2949120 | tf_op jit(solution)/shard_map/dot_general | solution.py:18
  96.3 2.2 %fusion.28 = f32[4,196,768]{2,1,0:T(8,128)} fusion(f32[4,196,16]{1,2,0:T(8,128)S(1)} %copy-done.6, f32[4,196,16]{1,2,0:T(8,128)S(1)} %convolution_bitcast_fusion, bf16[768,16]{0,1:T(8,128)(2,1)S(1)} %copy-done.8, f32[4,196,16]{1,2,0:T(8,128)S(1)} %copy-done.5, f32[4,16]{1,0:T(4,128)S(1)} %get-tuple-element.18), kind=kOutput, calls=%fused_computation.38 | convolution fusion | flops 19355652 | bytes 2583808 | tf_op jit(solution)/shard_map/bms,ds->bmd/dot_general | solution.py:83
  98.4 3.7 %add_convert_fusion = bf16[4,196,768]{2,1,0:T(8,128)(2,1)} fusion(f32[4,196,768]{2,1,0:T(8,128)} %fusion.28, bf16[4,16,768]{2,1,0:T(8,128)(2,1)S(1)} %reshape.36, f32[4,16]{1,0:T(4,128)S(1)} %get-tuple-element.18, f32[4,196,16]{1,2,0:T(8,128)S(1)} %copy-done.4), kind=kOutput, calls=%fused_computation.8 | convolution fusion | flops 20509700 | bytes 3761408 | tf_op jit(solution)/shard_map/bms,bsd->bmd/dot_general | solution.py:81
  102.1 2.8 %copy.43 = bf16[4,196,768]{2,0,1:T(4,128)(2,1)} copy(bf16[4,196,768]{2,1,0:T(8,128)(2,1)} %add_convert_fusion) | data formatting | bytes 2408448
  104.9 30.5 %all-gather.3.cloned.1.call-done = f32[24576,16]{0,1:T(8,128)} async-done(((f32[768,16]{0,1:T(8,128)}), f32[24576,16]{0,1:T(8,128)}) %all-gather.3.cloned.1.call-update) | async-done | bytes 1572880 | tf_op jit(solution)/shard_map/all_gather | solution.py:86
  138.0 3.9 %reshape_bitcast_fusion = bf16[1,1536,384]{1,0,2:T(2,128)(2,1)} fusion(bf16[384,1536]{1,0:T(8,128)(2,1)} %reduce-scatter.10.cloned.1.call-done), kind=kLoop, calls=%fused_computation.10 | loop fusion | bytes 2359296
  141.9 6.4 %copy.45 = bf16[1,1536,384]{2,1,0:T(8,128)(2,1)} copy(bf16[1,1536,384]{1,0,2:T(2,128)(2,1)} %reshape_bitcast_fusion) | data formatting | bytes 2359296
  148.4 14.2 %reduce-scatter.8.cloned.1.call-done = bf16[1,384,1536]{2,1,0:T(8,128)(2,1)} async-done(((bf16[1,768,1536]{2,1,0:T(8,128)(2,1)}), bf16[1,384,1536]{2,1,0:T(8,128)(2,1)}) %reduce-scatter.8.cloned.1.call-update) | async-done | bytes 1179664 | tf_op jit(solution)/shard_map/reduce_scatter | solution.py:63
  (52 shorter events, 21.3 us)
Async XLA Ops:
  8.0 31.7 %copy-start = (bf16[1,768,1536]{2,1,0:T(8,128)(2,1)S(1)}, bf16[1,768,1536]{2,1,0:T(8,128)(2,1)}, u32[]{:S(2)}) copy-start(bf16[1,768,1536]{2,1,0:T(8,128)(2,1)} %param.8) | copy-start | bytes 7077892
  9.9 12.7 %copy-start.3 = (f32[4,196,16]{1,2,0:T(8,128)}, f32[4,196,16]{1,2,0:T(8,128)S(1)}, u32[]{:S(2)}) copy-start(f32[4,196,16]{1,2,0:T(8,128)S(1)} %fusion.32) | copy-start | bytes 150532
  12.9 14.4 %all-to-all-start = ((bf16[4,8,2,768]{3,2,0,1:T(2,128)(2,1)}), bf16[4,8,2,768]{3,2,0,1:T(2,128)(2,1)S(1)}, u32[]{:S(2)}, u32[]{:S(2)}) async-start(bf16[4,8,2,768]{3,2,0,1:T(2,128)(2,1)} %copy.32), calls=%async_computation | async-start | bytes 196608 | tf_op jit(solution)/shard_map/all_to_all | solution.py:49
  27.3 10.4 %all-to-all-start.1 = ((bf16[4,8,2,768]{3,2,0,1:T(2,128)(2,1)}), bf16[4,8,2,768]{3,2,0,1:T(2,128)(2,1)S(1)}, u32[]{:S(2)}, u32[]{:S(2)}) async-start(bf16[4,8,2,768]{3,2,0,1:T(2,128)(2,1)} %copy.35), calls=%async_computation.1 | async-start | bytes 196608 | tf_op jit(solution)/shard_map/all_to_all | solution.py:48
  30.7 22.7 %reduce-scatter.6.cloned.1.call-start = ((), (), s32[]{:S(2)}) async-start(), calls=%async_computation.6 | async-start | bytes 589824 | tf_op jit(solution)/shard_map/reduce_scatter | solution.py:62
  32.7 7.5 %copy-start.2 = (bf16[128,768]{1,0:T(8,128)(2,1)}, bf16[128,768]{1,0:T(8,128)(2,1)S(1)}, u32[]{:S(2)}) copy-start(bf16[128,768]{1,0:T(8,128)(2,1)S(1)} %reshape_squeeze.6) | copy-start | bytes 589828
  39.7 1.7 copy-start.9
  45.1 2.7 %copy-start.10 = (bf16[4,16,768]{2,1,0:T(8,128)(2,1)S(1)}, bf16[4,16,768]{2,1,0:T(8,128)(2,1)}, u32[]{:S(2)}) copy-start(bf16[4,16,768]{2,1,0:T(8,128)(2,1)} %param.10) | copy-start | bytes 294916
  47.8 13.1 %copy-start.7 = (f32[4,196,16]{1,2,0:T(8,128)S(1)}, f32[4,196,16]{1,2,0:T(8,128)}, u32[]{:S(2)}) copy-start(f32[4,196,16]{1,2,0:T(8,128)} %get-tuple-element.17) | copy-start | bytes 150532
  55.1 12.8 %all-to-all-start.2 = ((bf16[32,1,2,768]{3,2,1,0:T(2,128)(2,1)}), bf16[32,1,2,768]{3,2,1,0:T(2,128)(2,1)S(1)}, u32[]{:S(2)}, u32[]{:S(2)}) async-start(bf16[32,1,2,768]{3,2,1,0:T(2,128)(2,1)} %copy.38), calls=%async_computation.3 | async-start | bytes 196608 | tf_op jit(solution)/shard_map/all_to_all | solution.py:70
  60.8 74.6 %all-gather.3.cloned.1.call-start = ((), (), s32[]{:S(2)}) async-start(), calls=%async_computation.8 | async-start | bytes 1622016 | tf_op jit(solution)/shard_map/all_gather | solution.py:86
  72.3 65.7 %reduce-scatter.10.cloned.1.call-start = ((), (), s32[]{:S(2)}) async-start(), calls=%async_computation.9 | async-start | bytes 3538944
  92.1 1.0 copy-start.1
  92.2 70.4 %reduce-scatter.8.cloned.1.call-start = ((), (), s32[]{:S(2)}) async-start(), calls=%async_computation.7 | async-start | bytes 3538944 | tf_op jit(solution)/shard_map/reduce_scatter | solution.py:63
  95.4 0.9 copy-start.5
  95.4 0.9 copy-start.6
  95.4 0.9 copy-start.8
  96.3 2.2 %copy-start.4 = (f32[4,196,16]{1,2,0:T(8,128)S(1)}, f32[4,196,16]{1,2,0:T(8,128)}, u32[]{:S(2)}) copy-start(f32[4,196,16]{1,2,0:T(8,128)} %copy-done.3) | copy-start | bytes 150532
Sparse Core Ops, SparseCore 0:
  47.9 5.4 reduce-scatter.5
  72.4 62.9 all-gather.2
Sparse Core Ops, SparseCore 1:
  92.3 32.9 reduce-scatter.9
  127.8 34.7 reduce-scatter.7
